TPU v7x, 32 devices: a whole 2x2x4 slice. The times are simulated.
32 devices in a mesh: groups: 2 (over y), coef: 4 (over x, core), slab: 4 (over z).
Axes of the slice: x: 2, y: 2, z: 4, core: 2. Of those that a mesh axis runs over, the one named last changes fastest.
Arguments:
- coefficients: float32 [896, 32768], P('coef', ('groups', 'slab')), parts along dimension 1, may hold values from -6 to 6
- measured: float32 [16, 4, 64, 256], P('groups', 'slab'), parts along dimension 0, may hold values from -6 to 6
- ray_voxels: int32 [8, 64, 128], replicated, may hold values from 0 to 4095
- ray_weights: int32 [8, 64, 128], replicated, may hold values from 1 to 63
- angle_ids: int32 [8], replicated, may hold values from 0 to 15
- angle_table: bfloat16 [16, 896, 256], P(None, 'coef'), may hold values from -0.1875 to 0.1875
- harmonics: bfloat16 [896, 2048], P('coef'), may hold values from -0.1875 to 0.1875
Outputs:
- updated: float32 [896, 32768], P('coef', ('groups', 'slab')), parts along dimension 1
- residual: float32 [16, 4, 64, 256], P('groups', 'slab', None, 'coef'), parts along dimension 0
There are 2 independent parts, one for each index of `groups`. A program takes and returns all parts, laid end to end along the dimension named above; an argument that names none is the same for every part. Nothing has to cross between parts.
All inputs are finite; a program needn't handle non-finite values.
Results may differ from a plain program's by a relative error of at most 0.0034.
Values may be sent and summed in bfloat16 or wider, within the bound.
A program may use at most 64 MiB of HBM per device.

v0:
```python
import jax
import jax.numpy as jnp
from jax import lax
from jax.sharding import PartitionSpec as P

NG = 64


def build_matrix(ray_voxels, ray_weights):
    shape_all = ray_voxels.shape
    side_count = NG
    high_part = ray_voxels // side_count
    low_part = ray_voxels % side_count
    positions = jnp.arange(side_count, dtype=jnp.int32)
    values = (ray_weights.astype(jnp.float32) / 256.0).astype(jnp.bfloat16)
    high_table = jnp.where(
        high_part[..., None] == positions, values[..., None], jnp.zeros((), jnp.bfloat16)
    )
    low_table = (low_part[..., None] == positions).astype(jnp.bfloat16)
    high_flat = high_table.reshape(shape_all[0] * shape_all[1], shape_all[2], side_count)
    low_flat = low_table.reshape(shape_all[0] * shape_all[1], shape_all[2], side_count)
    product = lax.dot_general(
        high_flat, low_flat, (((1,), (1,)), ((0,), (0,))), preferred_element_type=jnp.float32
    )
    return product.astype(jnp.bfloat16).reshape(shape_all[0], shape_all[1], side_count * side_count)


def select_angles(angle_ids, angle_table):
    entries = angle_table.shape[0]
    onehot = (angle_ids[:, None] == jnp.arange(entries)[None, :]).astype(jnp.bfloat16)
    flat_table = angle_table.reshape(entries, -1)
    picked = jnp.dot(onehot, flat_table, preferred_element_type=jnp.float32)
    return picked.astype(jnp.bfloat16).reshape((angle_ids.shape[0],) + angle_table.shape[1:])


def body(coefficients, measured, ray_voxels, ray_weights, angle_ids, angle_table, harmonics):
    coef_local = coefficients.shape[0]
    layers = coefficients.shape[1] // (NG * NG)
    system_matrix = build_matrix(ray_voxels, ray_weights)
    chosen = select_angles(angle_ids, angle_table)
    coef_half = coefficients.astype(jnp.bfloat16)
    stacked_rows = coef_half.reshape(coef_local, layers, NG * NG)
    ray_totals = jnp.einsum(
        "dmj,hqj->dqmh", system_matrix, stacked_rows, preferred_element_type=jnp.float32
    ).astype(jnp.bfloat16)
    partial_value = jnp.einsum(
        "azrk,akc->azrc", ray_totals, chosen, preferred_element_type=jnp.float32
    )
    chan_width = measured.shape[3] // lax.axis_size("coef")
    chan_start = lax.axis_index("coef") * chan_width
    predicted = lax.psum_scatter(partial_value, "coef", scatter_dimension=3, tiled=True)
    residual = predicted - lax.dynamic_slice_in_dim(measured, chan_start, chan_width, 3)
    resid_half = residual.astype(jnp.bfloat16)
    backward_projection = jnp.einsum(
        "azrc,akc->azrk",
        lax.all_gather(resid_half, "coef", axis=3, tiled=True),
        chosen,
        preferred_element_type=jnp.float32,
    )
    backward_half = backward_projection.astype(jnp.bfloat16)
    misfit_gradient = jnp.einsum(
        "qci,qbcy->ybi", system_matrix, backward_half, preferred_element_type=jnp.float32
    )
    misfit_gradient = misfit_gradient.reshape(coef_local, layers * NG * NG)
    grid_rows = coef_half.reshape(coef_local, layers * NG, NG)
    blocks = lax.all_to_all(grid_rows, "coef", split_axis=1, concat_axis=0, tiled=True)
    width_all, row_span, item_count = blocks.shape
    flat_cols = blocks.reshape(width_all, row_span * item_count)
    orient_field = lax.dot_general(
        flat_cols,
        lax.all_gather(harmonics, "coef", axis=0, tiled=True),
        (((0,), (0,)), ((), ())),
        preferred_element_type=jnp.float32,
    )
    slope_half = (-jax.nn.sigmoid(-orient_field)).astype(jnp.bfloat16)
    reg_grad = lax.dot_general(
        lax.all_gather(harmonics, "coef", axis=0, tiled=True),
        slope_half,
        (((1,), (1,)), ((), ())),
        preferred_element_type=jnp.float32,
    )
    reg_grad = reg_grad.reshape(width_all, row_span, item_count)
    reg_grad = lax.all_to_all(reg_grad, "coef", split_axis=0, concat_axis=1, tiled=True)
    reg_grad = reg_grad.reshape(coef_local, layers * NG * NG)
    updated = coefficients - 0.5 * misfit_gradient - 0.5 * reg_grad
    return (updated, residual)


def solution(mesh):
    in_specs = (
        P("coef", ("groups", "slab")),
        P("groups", "slab", None, None),
        P(),
        P(),
        P(),
        P(None, "coef", None),
        P("coef", None),
    )
    out_specs = (P("coef", ("groups", "slab")), P("groups", "slab", None, "coef"))
    return jax.shard_map(body, mesh=mesh, in_specs=in_specs, out_specs=out_specs, check_vma=False)
```

profile of v0, /device:TPU:9, one launch (start us, length us, event | category | flops | bytes accessed | tf_op | source)
XLA Modules:
  0.0 228.0 jit_solution(1820628051874065335)
XLA Ops:
  7.9 2.3 %convert_element_type.36 = bf16[224,4096]{1,0:T(8,128)(2,1)S(1)} convert(f32[224,4096]{1,0:T(8,128)} %param.7) | non-fusion elementwise | flops 917504 | bytes 5505024 | tf_op jit(solution)/shard_map/convert_element_type | solution.py:41
  10.2 2.5 %copy.37 = bf16[224,4096]{0,1:T(8,128)(2,1)} copy(bf16[224,4096]{1,0:T(8,128)(2,1)S(1)} %convert_element_type.36) | data formatting | bytes 3670016 | tf_op jit(solution)/shard_map/convert_element_type | solution.py:41
  12.7 4.3 %all-to-all-start = ((bf16[224,64,64]{0,2,1:T(8,128)(2,1)}), bf16[224,64,64]{0,2,1:T(8,128)(2,1)S(1)}, u32[]{:S(2)}, u32[]{:S(2)}) async-start(bf16[224,64,64]{0,2,1:T(8,128)(2,1)} %bitcast.58), calls=%async_computation | async-start | bytes 4194304 | tf_op jit(solution)/shard_map/all_to_all | solution.py:66
  17.2 44.1 %all-to-all-done = bf16[224,64,64]{0,2,1:T(8,128)(2,1)S(1)} async-done(((bf16[224,64,64]{0,2,1:T(8,128)(2,1)}), bf16[224,64,64]{0,2,1:T(8,128)(2,1)S(1)}, u32[]{:S(2)}, u32[]{:S(2)}) %all-to-all-start) | async-done | bytes 1835040 | tf_op jit(solution)/shard_map/all_to_all | solution.py:66
  61.3 3.1 %copy.53 = bf16[224,4,16,64]{0,1,3,2:T(4,128)(2,1)} copy(bf16[224,4,16,64]{0,3,2,1:T(8,128)(2,1)S(1)} %bitcast.57) | data formatting | bytes 3670016 | tf_op jit(solution)/shard_map/all_to_all | solution.py:66
  64.4 3.9 %reshape.62 = bf16[896,1024]{0,1:T(8,128)(2,1)S(1)} reshape(bf16[4,224,16,64]{1,0,3,2:T(4,128)(2,1)} %bitcast.59) | data formatting | bytes 3670016 | tf_op jit(solution)/shard_map/reshape | solution.py:68
  68.3 13.8 %fusion.13 = f32[1024,896]{1,0:T(8,128)} fusion(bf16[896,2048]{1,0:T(8,128)(2,1)} %all-gather.2.cloned.1.call-done, bf16[896,1024]{0,1:T(8,128)(2,1)S(1)} %reshape.62), kind=kOutput, calls=%fused_computation.15 | convolution fusion | flops 7524581376 | bytes 9175040 | tf_op jit(solution)/shard_map/dot_general | solution.py:76
  82.2 7.7 %copy.39 = f32[896,16,64]{2,1,0:T(8,128)} copy(f32[896,16,64]{0,2,1:T(8,128)} %bitcast.64) | data formatting | bytes 7340032 | tf_op jit(solution)/shard_map/reshape | solution.py:82
  89.8 7.8 %reshape.68 = f32[4,1,229376]{2,1,0:T(1,128)} reshape(f32[896,16,64]{2,1,0:T(8,128)} %copy.39) | data formatting | bytes 7340032
  97.6 5.7 %all-to-all-start.1 = ((f32[4,1,229376]{2,1,0:T(1,128)}), f32[4,1,229376]{2,1,0:T(1,128)}, u32[]{:S(2)}, u32[]{:S(2)}) async-start(f32[4,1,229376]{2,1,0:T(1,128)} %reshape.68), calls=%async_computation.1 | async-start | bytes 7340032 | tf_op jit(solution)/shard_map/all_to_all | solution.py:83
  103.4 6.6 %fusion.5 = bf16[512,64,64]{2,1,0:T(8,128)(2,1)} fusion(s32[512,128]{1,0:T(8,128)S(1)} %bitcast.68, s32[512,128]{1,0:T(8,128)S(1)} %bitcast.67, bf16[512,128]{1,0:T(8,128)(2,1)S(1)} %bitcast.70), kind=kOutput, calls=%fused_computation.8 | convolution fusion | flops 551550976 | bytes 4849664 | tf_op jit(solution)/shard_map/dot_general | solution.py:22
  110.0 12.0 %reshape.57 = bf16[8,64,4096]{2,1,0:T(8,128)(2,1)} reshape(bf16[512,64,64]{2,1,0:T(8,128)(2,1)} %fusion.5) | data formatting | bytes 8388608 | tf_op jit(solution)/shard_map/reshape | solution.py:25
  122.0 2.7 %copy.46 = bf16[2,8,224,256]{3,1,2,0:T(8,128)(2,1)S(1)} copy(bf16[2,8,224,256]{3,2,1,0:T(8,128)(2,1)} %bitcast.65) | data formatting | bytes 3670016
  125.2 3.8 %convolution_bitcast_fusion.1 = f32[8,1,64,256]{3,2,0,1:T(8,128)S(1)} fusion(bf16[8,224,256]{2,0,1:T(8,128)(2,1)S(1)} %bitcast.62, bf16[8,64,4096]{2,1,0:T(8,128)(2,1)} %reshape.57, bf16[224,4096]{1,0:T(8,128)(2,1)S(1)} %copy-done.1), kind=kOutput, calls=%fused_computation.20 | convolution fusion | flops 998359040 | bytes 7471104 | tf_op jit(solution)/shard_map/azrk,akc->azrc/dot_general | solution.py:46
  130.6 22.6 %reduce-scatter.4.cloned.1.call-done = f32[64,512]{1,0:T(8,128)} async-done(((f32[256,512]{1,0:T(8,128)}), f32[64,512]{1,0:T(8,128)}) %reduce-scatter.4.cloned.1.call-update) | async-done | bytes 131088
  155.4 7.5 %all_gather.7 = bf16[8,1,64,256]{2,0,1,3:T(8,128)(2,1)S(1)} all-gather(bf16[8,1,64,64]{2,0,1,3:T(8,128)(2,1)S(1)} %copy.34), channel_id=1, replica_groups=mesh['groups'=2,'coef'=4,'slab'=4] {'coef'}, dimensions={3}, use_global_device_ids=true | all-gather | bytes 327680 | tf_op jit(solution)/shard_map/all_gather | solution.py:56
  163.7 13.6 %reduce = f32[4,229376]{1,0:T(4,128)} reduce(f32[4,1,229376]{2,1,0:T(1,128)} %all-to-all-done.1, f32[]{:T(128)} %broadcast.44), dimensions={1}, to_apply=%all_to_all.21.reduce_sub_computation | reduce | bytes 7340036 | tf_op jit(solution)/shard_map/all_to_all | solution.py:83
  177.4 8.4 %reshape.69 = f32[896,16,64]{2,1,0:T(8,128)} reshape(f32[4,229376]{1,0:T(4,128)} %reduce) | data formatting | bytes 7340032
  185.7 6.5 %copy.40 = f32[896,16,64]{0,2,1:T(8,128)} copy(f32[896,16,64]{2,1,0:T(8,128)} %reshape.69) | data formatting | bytes 7340032 | tf_op jit(solution)/shard_map/all_to_all | solution.py:83
  192.3 4.2 %broadcast_multiply_fusion = f32[896,16,64]{0,2,1:T(8,128)} fusion(f32[896,16,64]{0,2,1:T(8,128)} %copy.40), kind=kLoop, calls=%fused_computation.19 | loop fusion | flops 917504 | bytes 7340032 | tf_op jit(solution)/shard_map/mul | solution.py:85
  196.5 6.4 %mul.21 = f32[4,224,16,64]{1,0,3,2:T(4,128)} reshape(f32[896,16,64]{0,2,1:T(8,128)} %broadcast_multiply_fusion) | data formatting | bytes 7340032 | tf_op jit(solution)/shard_map/mul | solution.py:85
  202.9 5.0 %copy.41 = f32[224,4,16,64]{0,3,2,1:T(8,128)} copy(f32[224,4,16,64]{0,1,3,2:T(4,128)} %bitcast.55) | data formatting | bytes 7340032 | tf_op jit(solution)/shard_map/mul | solution.py:85
  207.9 5.5 %copy.42 = f32[224,4096]{1,0:T(8,128)} copy(f32[224,4096]{0,1:T(8,128)} %bitcast.56) | data formatting | bytes 7340032 | tf_op jit(solution)/shard_map/mul | solution.py:85
  213.4 7.8 %fusion.10 = f32[224,4096]{1,0:T(8,128)} fusion(f32[224,4096]{1,0:T(8,128)} %copy.42, f32[224,4096]{1,0:T(8,128)} %param.7, bf16[8,64,4096]{2,1,0:T(8,128)(2,1)} %reshape.57, bf16[8,224,256]{2,0,1:T(8,128)(2,1)S(1)} %bitcast.63, bf16[8,1,64,256]{3,2,0,1:T(8,128)(2,1)S(1)} %copy.35), kind=kOutput, calls=%fused_computation.12 | convolution fusion | flops 1001111552 | bytes 16384000 | tf_op jit(solution)/shard_map/qci,qbcy->ybi/dot_general | solution.py:61
  (29 shorter events, 6.0 us)
Async XLA Ops:
  7.2 61.2 %all-gather.2.cloned.1.call-start = ((), (), s32[]{:S(2)}) async-start(), calls=%async_computation.3 | async-start | bytes 4587520 | tf_op jit(solution)/shard_map/all_gather | solution.py:77
  10.2 2.5 %copy-start = (bf16[224,4096]{1,0:T(8,128)(2,1)}, bf16[224,4096]{1,0:T(8,128)(2,1)S(1)}, u32[]{:S(2)}) copy-start(bf16[224,4096]{1,0:T(8,128)(2,1)S(1)} %convert_element_type.36) | copy-start | bytes 5505028
  10.2 6.8 %copy-start.3 = (s32[8,64,128]{2,1,0:T(8,128)S(1)}, s32[8,64,128]{2,1,0:T(8,128)}, u32[]{:S(2)}) copy-start(s32[8,64,128]{2,1,0:T(8,128)} %param.10) | copy-start | bytes 786436
  10.2 6.8 %copy-start.2 = (s32[8,64,128]{2,1,0:T(8,128)S(1)}, s32[8,64,128]{2,1,0:T(8,128)}, u32[]{:S(2)}) copy-start(s32[8,64,128]{2,1,0:T(8,128)} %param.9) | copy-start | bytes 786436
  12.7 48.6 %all-to-all-start = ((bf16[224,64,64]{0,2,1:T(8,128)(2,1)}), bf16[224,64,64]{0,2,1:T(8,128)(2,1)S(1)}, u32[]{:S(2)}, u32[]{:S(2)}) async-start(bf16[224,64,64]{0,2,1:T(8,128)(2,1)} %bitcast.58), calls=%async_computation | async-start | bytes 4194304 | tf_op jit(solution)/shard_map/all_to_all | solution.py:66
  97.6 65.6 %all-to-all-start.1 = ((f32[4,1,229376]{2,1,0:T(1,128)}), f32[4,1,229376]{2,1,0:T(1,128)}, u32[]{:S(2)}, u32[]{:S(2)}) async-start(f32[4,1,229376]{2,1,0:T(1,128)} %reshape.68), calls=%async_computation.1 | async-start | bytes 7340032 | tf_op jit(solution)/shard_map/all_to_all | solution.py:83
  103.4 49.8 %reduce-scatter.4.cloned.1.call-start = ((), (), s32[]{:S(2)}) async-start(), calls=%async_computation.4 | async-start | bytes 655360
  122.0 2.7 %copy-start.5 = (s32[8]{0:T(128)S(1)}, s32[8]{0:T(128)}, u32[]{:S(2)}) copy-start(s32[8]{0:T(128)} %param.11) | copy-start | bytes 100
  122.0 3.1 %copy-start.1 = (bf16[224,4096]{1,0:T(8,128)(2,1)S(1)}, bf16[224,4096]{1,0:T(8,128)(2,1)}, u32[]{:S(2)}) copy-start(bf16[224,4096]{1,0:T(8,128)(2,1)} %copy-done) | copy-start | bytes 5505028
  129.0 25.3 %copy-start.4 = (f32[8,1,64,256]{3,2,1,0:T(8,128)S(1)}, f32[8,1,64,256]{3,2,1,0:T(8,128)}, u32[]{:S(2)}) copy-start(f32[8,1,64,256]{3,2,1,0:T(8,128)} %param.8) | copy-start | bytes 1572868
Sparse Core Ops, SparseCore 0:
  9.5 52.7 all-gather.1
  130.7 22.4 reduce-scatter.3
where the time goes:
time: 230 us; the launch traced here: 228 us
  local copies, waits for them, and re-layouts  75 us (33%)
  waiting for transfers between devices  67.5 us (29%)
  matrix products  32.5 us (14%)
  other arithmetic  21.3 us (9%)
  between operations  14.2 us (6%)
  starting transfers between devices  10 us (4%)
  blocking collectives  7.5 us (3%)
    all_to_all x1, waiting for transfers between devices, body(): lax.all_to_all(grid_rows, 'coef', split_axis=1, concat_axis=0, tiled=True)  44.1 us
    unnamed x3, waiting for transfers between devices  23.3 us
    unnamed x19, local copies, waits for them, and re-layouts  21.5 us
    mul x3, local copies, waits for them, and re-layouts, body(): updated = coefficients - 0.5 * misfit_gradient - 0.5 * reg_grad  16.9 us
    dot_general x1, matrix products, body(): lax.dot_general(lax.all_gather(harmonics, 'coef', axis=0, tiled=True), sl...  13.8 us
    all_to_all x1, other arithmetic, body(): lax.all_to_all(reg_grad, 'coef', split_axis=0, concat_axis=1, tiled=True)  13.6 us
    reshape x1, local copies, waits for them, and re-layouts, build_matrix(): product.astype(jnp.bfloat16)  12 us
    dot_general x1, matrix products, body(): jnp.einsum('qci,qbcy->ybi', system_matrix, backward_half, preferred_eleme...  7.78 us
  transfers between devices with their start and end apart: 4, of which 2 were waited for; matrix products, arithmetic and copies ran while one was open for 18% of the time, Pallas kernels for 0%

commit v1 on v0

v1 whole, which is shorter than its diff:
```python
import functools

import jax
import jax.numpy as jnp
from jax import lax
from jax.experimental import pallas as pl
from jax.experimental.pallas import tpu as pltpu
from jax.sharding import PartitionSpec as P

NG = 64
LANES = 128
BF = jnp.bfloat16
F32 = jnp.float32
NT = (((1,), (1,)), ((), ()))
TN = (((0,), (0,)), ((), ()))
NN = (((1,), (0,)), ((), ()))


def dot(a, b, dims):
    return lax.dot_general(a, b, dims, preferred_element_type=F32)


def kernel(n, tiles, coef_hbm, meas_hbm, vox_ref, wgt_ref, ids_ref, table_hbm, harm_hbm,
           upd_hbm, resid_ref,
           coef, coef_bf, meas, table, harm, recv, matrix, prod, rays, ray_acc, parts, inbox,
           bp_t, racc, rsend, rrecv,
           load_sem, out_sem, hsend, hrecv, csend, crecv, psend, precv, gsend, grecv):
    me = lax.axis_index("coef")
    cl, width = coef.shape
    share = width // n
    vt = share // tiles
    angles, layers, nrays, chans = meas.shape
    plane = NG * NG
    orient = harm.shape[2]
    steps = n.bit_length() - 1
    sibling = me + 1 - 2 * lax.rem(me, 2)

    loads = [
        pltpu.make_async_copy(coef_hbm, coef, load_sem.at[0]),
        pltpu.make_async_copy(harm_hbm, harm.at[me], load_sem.at[1]),
        pltpu.make_async_copy(table_hbm, table, load_sem.at[2]),
        pltpu.make_async_copy(meas_hbm, meas, load_sem.at[3]),
    ]
    for item in loads:
        item.start()

    barrier = pltpu.get_barrier_semaphore()
    for d in range(1, n):
        pl.semaphore_signal(barrier, inc=1, device_id={"coef": lax.rem(me + d, n)},
                            device_id_type=pl.DeviceIdType.MESH)
    pl.semaphore_wait(barrier, n - 1)

    def remote(src, dst, ssem, rsem, target):
        return pltpu.make_async_remote_copy(
            src_ref=src, dst_ref=dst, send_sem=ssem, recv_sem=rsem,
            device_id={"coef": target}, device_id_type=pl.DeviceIdType.MESH)

    harm_direct = []
    for e in range(1, n // 2):
        harm_direct.append(remote(harm_hbm, harm.at[me], hsend.at[0, e], hrecv.at[me],
                                  lax.rem(me + 2 * e, n)))
        harm_direct[-1].start()
    harm_sib = remote(harm_hbm, harm.at[me], hsend.at[0, 0], hrecv.at[me], sibling)
    harm_sib.start()

    loads[0].wait()
    coef_copies = []
    for t in range(tiles):
        for d in range(n):
            j = lax.rem(me + d, n)
            at = pl.multiple_of(j * share + t * vt, LANES)
            block = coef[:, pl.ds(at, vt)].astype(BF)
            coef_bf[:, pl.ds(at, vt)] = block
            if d == 0:
                recv[t, me] = block
    for t in range(tiles):
        for d in range(1, n):
            j = lax.rem(me + d, n)
            at = pl.multiple_of(j * share + t * vt, LANES)
            item = remote(coef_bf.at[:, pl.ds(at, vt)], recv.at[t, me], csend.at[t, d],
                          crecv.at[t, me], j)
            item.start()
            coef_copies.append(item)

    samples = vox_ref.shape[1]
    rows_hi = plane // LANES
    pos_lo = lax.broadcasted_iota(jnp.int32, (LANES, samples), 0)
    pos_hi = lax.broadcasted_iota(jnp.int32, (rows_hi, samples), 0)

    def build(g, carry):
        r0 = pl.multiple_of(g * 16, 16)
        vox = vox_ref[pl.ds(r0, 16), :]
        wgt = wgt_ref[pl.ds(r0, 16), :].astype(F32) * (1.0 / 256.0)
        high = vox // LANES
        low = vox - high * LANES
        for i in range(16):
            oh_hi = jnp.where(high[i:i + 1, :] == pos_hi, wgt[i:i + 1, :], 0.0).astype(BF)
            oh_lo = jnp.where(low[i:i + 1, :] == pos_lo, 1.0, 0.0).astype(BF)
            prod[pl.ds(i * rows_hi, rows_hi), :] = dot(oh_hi, oh_lo, NT)
        for h in range(rows_hi):
            matrix[pl.ds(r0, 16), pl.ds(h * LANES, LANES)] = prod[
                pl.ds(h, 16, stride=rows_hi), :].astype(BF)
        return carry

    lax.fori_loop(0, (angles * nrays) // 16, build, 0)

    kc = 512
    loads[2].wait()
    for z in range(layers):
        ray_acc[...] = jnp.zeros_like(ray_acc)

        def project(i, carry, z=z):
            at = pl.multiple_of(i * kc, kc)
            ray_acc[...] += dot(matrix[:, pl.ds(at, kc)],
                                coef_bf[:, pl.ds(pl.multiple_of(z * plane + i * kc, kc), kc)], NT)
            return carry

        lax.fori_loop(0, plane // kc, project, 0)
        rays[...] = ray_acc[...].astype(BF)
        for a in range(angles):
            parts[0, a, z] = dot(rays[a * nrays:(a + 1) * nrays, :], table[ids_ref[a]], NN)

    def swap(s):
        bit = 1 << s
        partner = me + (1 - 2 * lax.rem(me // bit, 2)) * bit
        return remote(parts.at[s], inbox.at[s], psend.at[s], precv.at[s], partner)

    swaps = [swap(s) for s in range(steps)]
    swaps[0].start()

    loads[1].wait()
    forwards = []
    for e in range(1, n // 2):
        j = lax.rem(me + 2 * e, n)
        remote(harm_hbm, harm.at[j], hsend.at[0, e], hrecv.at[j], j).wait_recv()
        item = remote(harm.at[j], harm.at[j], hsend.at[1, e], hrecv.at[j], sibling)
        item.start()
        forwards.append(item)
    for e in range(n // 2):
        j = lax.rem(sibling + 2 * e, n)
        remote(harm.at[j], harm.at[j], hsend.at[1, 0], hrecv.at[j], sibling).wait_recv()

    def finish_swap(s):
        swaps[s].wait()
        parts[s + 1] = parts[s] + inbox[s]
        if s + 1 < steps:
            swaps[s + 1].start()

    oc = 512
    back = []
    done_swaps = 0
    for t in range(tiles):
        for d in range(1, n):
            j = lax.rem(me + d, n)
            remote(coef_bf.at[:, pl.ds(0, vt)], recv.at[t, j], csend.at[t, d],
                   crecv.at[t, j], j).wait_recv()
        racc[...] = jnp.zeros_like(racc)

        def penalty(i, carry, t=t):
            at = pl.multiple_of(i * oc, oc)
            field = dot(harm[0, :, pl.ds(at, oc)], recv[t, 0], TN)
            for j in range(1, n):
                field += dot(harm[j, :, pl.ds(at, oc)], recv[t, j], TN)
            slope = (-1.0 / (1.0 + jnp.exp(field))).astype(BF)
            for j in range(n):
                racc[j] += dot(harm[j, :, pl.ds(at, oc)], slope, NN)
            return carry

        lax.fori_loop(0, orient // oc, penalty, 0)
        if done_swaps < steps:
            finish_swap(done_swaps)
            done_swaps += 1
        rsend[t] = racc[...].astype(BF)
        rrecv[t, me] = rsend[t, me]
        for d in range(1, n):
            j = lax.rem(me + d, n)
            item = remote(rsend.at[t, j], rrecv.at[t, me], gsend.at[t, d], grecv.at[t, me], j)
            item.start()
            back.append(item)
    while done_swaps < steps:
        finish_swap(done_swaps)
        done_swaps += 1

    loads[3].wait()
    resid_ref[...] = parts[steps] - meas[...]
    for z in range(layers):
        for a in range(angles):
            bp_t[:, a * nrays:(a + 1) * nrays] = dot(
                table[ids_ref[a]], resid_ref[a, z].astype(BF), NT).astype(BF)

        def gradient(i, carry, z=z):
            at = pl.multiple_of(i * kc, kc)
            to = pl.multiple_of(z * plane + i * kc, kc)
            coef[:, pl.ds(to, kc)] = coef[:, pl.ds(to, kc)] - 0.5 * dot(
                bp_t[...], matrix[:, pl.ds(at, kc)], NN)
            return carry

        lax.fori_loop(0, plane // kc, gradient, 0)

    outs = []
    for t in range(tiles):
        for d in range(n):
            j = lax.rem(me + d, n)
            if d > 0:
                remote(rsend.at[t, j], rrecv.at[t, j], gsend.at[t, d], grecv.at[t, j], j).wait_recv()
            at = pl.multiple_of(j * share + t * vt, LANES)
            coef[:, pl.ds(at, vt)] = coef[:, pl.ds(at, vt)] - 0.5 * rrecv[t, j].astype(F32)
            item = pltpu.make_async_copy(coef.at[:, pl.ds(at, vt)], upd_hbm.at[:, pl.ds(at, vt)],
                                         out_sem.at[t, d])
            item.start()
            outs.append(item)
    for item in harm_direct + [harm_sib] + forwards + coef_copies + back:
        item.wait_send()
    for item in outs:
        item.wait()


def body(coefficients, measured, ray_voxels, ray_weights, angle_ids, angle_table, harmonics):
    n = lax.axis_size("coef")
    cl, width = coefficients.shape
    angles, layers, nrays, chans = measured.shape
    rows = angles * nrays
    orient = harmonics.shape[1]
    share = width // n
    tiles = 2
    vt = share // tiles
    steps = n.bit_length() - 1
    any_spec = pl.BlockSpec(memory_space=pl.ANY)
    vmem_spec = pl.BlockSpec(memory_space=pltpu.VMEM)
    smem_spec = pl.BlockSpec(memory_space=pltpu.SMEM)
    dma = pltpu.SemaphoreType.DMA
    updated, residual = pl.pallas_call(
        functools.partial(kernel, n, tiles),
        out_shape=(jax.ShapeDtypeStruct(coefficients.shape, F32),
                   jax.ShapeDtypeStruct(measured.shape, F32)),
        in_specs=[any_spec, any_spec, vmem_spec, vmem_spec, smem_spec, any_spec, any_spec],
        out_specs=(any_spec, vmem_spec),
        scratch_shapes=[
            pltpu.VMEM((cl, width), F32),
            pltpu.VMEM((cl, width), BF),
            pltpu.VMEM(measured.shape, F32),
            pltpu.VMEM(angle_table.shape, BF),
            pltpu.VMEM((n, cl, orient), BF),
            pltpu.VMEM((tiles, n, cl, vt), BF),
            pltpu.VMEM((rows, NG * NG), BF),
            pltpu.VMEM((16 * (NG * NG // LANES), LANES), F32),
            pltpu.VMEM((rows, cl), BF),
            pltpu.VMEM((rows, cl), F32),
            pltpu.VMEM((steps + 1,) + measured.shape, F32),
            pltpu.VMEM((steps,) + measured.shape, F32),
            pltpu.VMEM((cl, rows), BF),
            pltpu.VMEM((n, cl, vt), F32),
            pltpu.VMEM((tiles, n, cl, vt), BF),
            pltpu.VMEM((tiles, n, cl, vt), BF),
            dma((4,)),
            dma((tiles, n)),
            dma((2, n)),
            dma((n,)),
            dma((tiles, n)),
            dma((tiles, n)),
            dma((steps,)),
            dma((steps,)),
            dma((tiles, n)),
            dma((tiles, n)),
        ],
        compiler_params=pltpu.CompilerParams(
            collective_id=0, has_side_effects=True, vmem_limit_bytes=60 * 1024 * 1024),
        name="step",
    )(coefficients, measured, ray_voxels.reshape(rows, -1), ray_weights.reshape(rows, -1),
      angle_ids, angle_table, harmonics)
    chan_width = chans // n
    residual = lax.dynamic_slice_in_dim(residual, lax.axis_index("coef") * chan_width, chan_width, 3)
    return updated, residual


def solution(mesh):
    in_specs = (
        P("coef", ("groups", "slab")),
        P("groups", "slab", None, None),
        P(),
        P(),
        P(),
        P(None, "coef", None),
        P("coef", None),
    )
    out_specs = (P("coef", ("groups", "slab")), P("groups", "slab", None, "coef"))
    return jax.shard_map(body, mesh=mesh, in_specs=in_specs, out_specs=out_specs, check_vma=False)
```

time: 230 us -> 84.7 us (0.37)
  Pallas kernels: 0 us -> 77.1 us
  local copies, waits for them, and re-layouts: 75 us -> 6.07 us
  waiting for transfers between devices: 67.5 us -> 0 us
  matrix products: 32.5 us -> 0 us
  other arithmetic: 21.3 us -> 0 us
  between operations: 14.2 us -> 0.65 us
  starting transfers between devices: 10 us -> 0 us
  blocking collectives: 7.5 us -> 0 us
    pallas_call x0 -> x1, Pallas kernels: none -> 77.1 us  [body(): pl.pallas_call(functools.partial(kernel, n, tiles), out_shape=(jax.ShapeD...]
    all_to_all x2 -> x0, waiting for transfers between devices: 44.1 us -> none  [the longest x1 44.1 us: body(): lax.all_to_all(grid_rows, 'coef', split_axis=1, concat_axis=0, tiled=True)]
    dot_general x5 -> x0, matrix products: 32.5 us -> none  [the longest x1 13.8 us: body(): lax.dot_general(lax.all_gather(harmonics, 'coef', axis=0, tiled=True), sl...]
    reshape x3 -> x0, local copies, waits for them, and re-layouts: 23.6 us -> none  [the longest x1 12 us: build_matrix(): product.astype(jnp.bfloat16)]
    unnamed x3 -> x0, waiting for transfers between devices: 23.3 us -> none
    unnamed x19 -> x1, local copies, waits for them, and re-layouts: 21.5 us -> 4.28 us
    mul x3 -> x0, local copies, waits for them, and re-layouts: 16.9 us -> none  [body(): updated = coefficients - 0.5 * misfit_gradient - 0.5 * reg_grad]
    all_to_all x1 -> x0, other arithmetic: 13.6 us -> none  [body(): lax.all_to_all(reg_grad, 'coef', split_axis=0, concat_axis=1, tiled=True)]
  transfers between devices with their start and end apart: 4 -> 0, of which waited for: 2 -> 0; matrix products, arithmetic and copies ran while one was open for 18% -> 0% of each run, Pallas kernels for 0% -> 0%
where the time goes in v1:
time: 84.7 us; the launch traced here: 83.8 us
  Pallas kernels  77.1 us (91%)
  local copies, waits for them, and re-layouts  6.07 us (7%)
    pallas_call x1, Pallas kernels, body(): pl.pallas_call(functools.partial(kernel, n, tiles), out_shape=(jax.ShapeD...  77.1 us
    unnamed x1, local copies, waits for them, and re-layouts  4.28 us
    dynamic_slice x1, local copies, waits for them, and re-layouts, body(): lax.dynamic_slice_in_dim(residual, lax.axis_index('coef') * chan_width, c...  1.8 us

profile of v1, /device:TPU:9, one launch (start us, length us, event | category | flops | bytes accessed | tf_op | source)
XLA Modules:
  0.0 83.8 jit_solution(7700881854276867920)
XLA Ops:
  0.6 77.1 %step.1 = (f32[224,4096]{1,0:T(8,128)}, f32[8,1,64,256]{3,2,1,0:T(8,128)}) custom-call(f32[224,4096]{1,0:T(8,128)} %coef_hbm.1, f32[8,1,64,256]{3,2,1,0:T(8,128)} %meas_hbm.1, s32[512,128]{1,0:T(8,128)} %bitcast.2, s32[512,128]{1,0:T(8,128)} %bitcast.3, s32[8]{0:T(128)} %ids_ref.1, bf16[16,224,256]{2,1,0:T(8,128)(2,1)} %table_hbm.1, bf16[224,2048]{1,0:T(8,128)(2,1)} %harm_hbm.1), custom_call_target="tpu_custom_call" | custom-call | tf_op jit(solution)/shard_map/step/pallas_call | solution.py:232
  77.7 1.8 %constant_dynamic-slice_fusion = f32[8,1,64,64]{3,2,1,0:T(8,128)} fusion(f32[8,1,64,256]{3,2,1,0:T(8,128)} %get-tuple-element.5, s32[]{:T(128)S(6)} %select_n.3), kind=kLoop, calls=%fused_computation | loop fusion | bytes 262148 | tf_op jit(solution)/shard_map/dynamic_slice | solution.py:272
  79.5 4.3 %copy.10 = f32[224,4096]{1,0:T(8,128)} copy(f32[224,4096]{1,0:T(8,128)} %get-tuple-element.8) | data formatting | bytes 7340032

commit v2 on v1

--- a/solution.py
+++ b/solution.py
@@ -20,12 +20,15 @@
     return lax.dot_general(a, b, dims, preferred_element_type=F32)
 
 
-def kernel(n, tiles, coef_hbm, meas_hbm, vox_ref, wgt_ref, ids_ref, table_hbm, harm_hbm,
+def kernel(n, slabs, split, tiles, coef_hbm, meas_hbm, vox_ref, wgt_ref, ids_ref, table_hbm, harm_hbm,
            upd_hbm, resid_ref,
-           coef, coef_bf, meas, table, harm, recv, matrix, prod, rays, ray_acc, parts, inbox,
+           coef, coef_bf, meas, table, harm, recv, matrix, prod, rays, ray_acc, part, half, inbox, full,
            bp_t, racc, rsend, rrecv,
-           load_sem, out_sem, hsend, hrecv, csend, crecv, psend, precv, gsend, grecv):
+           load_sem, out_sem, own_s, own_r, hx_s, hx_r, hz_s, hz_r, hy_s, hy_r, hs_s, hs_r,
+           csend, crecv, psend, precv, gsend, grecv):
     me = lax.axis_index("coef")
+    mz = lax.axis_index("slab")
+    my = lax.axis_index("groups") if split > 1 else 0
     cl, width = coef.shape
     share = width // n
     vt = share // tiles
@@ -45,23 +48,80 @@
         item.start()
 
     barrier = pltpu.get_barrier_semaphore()
-    for d in range(1, n):
-        pl.semaphore_signal(barrier, inc=1, device_id={"coef": lax.rem(me + d, n)},
-                            device_id_type=pl.DeviceIdType.MESH)
-    pl.semaphore_wait(barrier, n - 1)
-
-    def remote(src, dst, ssem, rsem, target):
+    for axis, index, size in (("coef", me, n), ("slab", mz, slabs), ("groups", my, split)):
+        for d in range(1, size):
+            pl.semaphore_signal(barrier, inc=1, device_id={axis: lax.rem(index + d, size)},
+                                device_id_type=pl.DeviceIdType.MESH)
+    pl.semaphore_wait(barrier, n + slabs + split - 3)
+
+    def remote(src, dst, ssem, rsem, target, axis="coef"):
         return pltpu.make_async_remote_copy(
             src_ref=src, dst_ref=dst, send_sem=ssem, recv_sem=rsem,
-            device_id={"coef": target}, device_id_type=pl.DeviceIdType.MESH)
-
-    harm_direct = []
-    for e in range(1, n // 2):
-        harm_direct.append(remote(harm_hbm, harm.at[me], hsend.at[0, e], hrecv.at[me],
-                                  lax.rem(me + 2 * e, n)))
-        harm_direct[-1].start()
-    harm_sib = remote(harm_hbm, harm.at[me], hsend.at[0, 0], hrecv.at[me], sibling)
-    harm_sib.start()
+            device_id={axis: target}, device_id_type=pl.DeviceIdType.MESH)
+
+    ow = orient // (slabs * split)
+    mates = [lax.rem(me + 2 * e, n) for e in range(1, n // 2)]
+    sib_mates = [lax.rem(sibling + 2 * e, n) for e in range(1, n // 2)]
+    sent = []
+
+    def cols(zi, yi):
+        return pl.ds(pl.multiple_of((zi * split + yi) * ow, LANES), ow)
+
+    def launch(*args):
+        item = remote(*args)
+        item.start()
+        sent.append(item)
+
+    def arrived(ref, sem):
+        remote(ref, ref, sem, sem, sibling).wait_recv()
+
+    def spread_y(b, zi):
+        piece = harm.at[b, :, cols(zi, my)]
+        for d in range(1, split):
+            to = lax.rem(my + d, split)
+            launch(piece, piece, hy_s.at[b, zi, to], hy_r.at[b, zi, my], to, "groups")
+
+    def to_sibling(b, zi, yi):
+        piece = harm.at[b, :, cols(zi, yi)]
+        launch(piece, piece, hs_s.at[b, zi, yi], hs_r.at[b, zi, yi], sibling)
+
+    for b in mates:
+        launch(harm_hbm.at[:, cols(mz, my)], harm.at[me, :, cols(mz, my)], hx_s.at[b],
+               hx_r.at[me], b)
+    launch(harm_hbm, harm.at[me], own_s.at[0], own_r.at[0], sibling)
+
+    def x_arrive():
+        for b in mates:
+            piece = harm.at[b, :, cols(mz, my)]
+            arrived(piece, hx_r.at[b])
+            for d in range(1, slabs):
+                to = lax.rem(mz + d, slabs)
+                launch(piece, piece, hz_s.at[b, to], hz_r.at[b, mz], to, "slab")
+            spread_y(b, mz)
+            to_sibling(b, mz, my)
+
+    def z_arrive(d):
+        zi = lax.rem(mz + d, slabs)
+        for b in mates:
+            arrived(harm.at[b, :, cols(zi, my)], hz_r.at[b, zi])
+            spread_y(b, zi)
+            to_sibling(b, zi, my)
+
+    def y_arrive():
+        for d in range(slabs):
+            zi = lax.rem(mz + d, slabs)
+            for b in mates:
+                for f in range(1, split):
+                    yi = lax.rem(my + f, split)
+                    arrived(harm.at[b, :, cols(zi, yi)], hy_r.at[b, zi, yi])
+                    to_sibling(b, zi, yi)
+
+    def sibling_arrive():
+        arrived(harm.at[sibling], own_r.at[0])
+        for b in sib_mates:
+            for zi in range(slabs):
+                for yi in range(split):
+                    arrived(harm.at[b, :, cols(zi, yi)], hs_r.at[b, zi, yi])
 
     loads[0].wait()
     coef_copies = []
@@ -102,7 +162,16 @@
                 pl.ds(h, 16, stride=rows_hi), :].astype(BF)
         return carry
 
-    lax.fori_loop(0, (angles * nrays) // 16, build, 0)
+    groups16 = (angles * nrays) // 16
+    parts = 4
+    for q in range(parts):
+        lax.fori_loop(q * groups16 // parts, (q + 1) * groups16 // parts, build, 0)
+        if q == 0:
+            x_arrive()
+        elif q < slabs:
+            z_arrive(q)
+    for q in range(parts, slabs):
+        z_arrive(q)
 
     kc = 512
     loads[2].wait()
@@ -118,37 +187,38 @@
         lax.fori_loop(0, plane // kc, project, 0)
         rays[...] = ray_acc[...].astype(BF)
         for a in range(angles):
-            parts[0, a, z] = dot(rays[a * nrays:(a + 1) * nrays, :], table[ids_ref[a]], NN)
+            part[a, z] = dot(rays[a * nrays:(a + 1) * nrays, :], table[ids_ref[a]], NN)
+
+    ha = angles // 2
+    par = lax.rem(me, 2)
+    mine, other = pl.ds(par * ha, ha), pl.ds((1 - par) * ha, ha)
 
     def swap(s):
+        if s == 0:
+            return remote(part.at[other], inbox.at[0], psend.at[0], precv.at[0], sibling)
+        if s == steps:
+            return remote(half.at[s - 1], full.at[mine], psend.at[s], precv.at[s], sibling)
         bit = 1 << s
         partner = me + (1 - 2 * lax.rem(me // bit, 2)) * bit
-        return remote(parts.at[s], inbox.at[s], psend.at[s], precv.at[s], partner)
-
-    swaps = [swap(s) for s in range(steps)]
+        return remote(half.at[s - 1], inbox.at[s], psend.at[s], precv.at[s], partner)
+
+    swaps = [swap(s) for s in range(steps + 1)]
     swaps[0].start()
 
+    def finish_swap(s):
+        swaps[s].wait_recv()
+        if s < steps:
+            half[s] = (part[mine] if s == 0 else half[s - 1]) + inbox[s]
+            swaps[s + 1].start()
+
     loads[1].wait()
-    forwards = []
-    for e in range(1, n // 2):
-        j = lax.rem(me + 2 * e, n)
-        remote(harm_hbm, harm.at[j], hsend.at[0, e], hrecv.at[j], j).wait_recv()
-        item = remote(harm.at[j], harm.at[j], hsend.at[1, e], hrecv.at[j], sibling)
-        item.start()
-        forwards.append(item)
-    for e in range(n // 2):
-        j = lax.rem(sibling + 2 * e, n)
-        remote(harm.at[j], harm.at[j], hsend.at[1, 0], hrecv.at[j], sibling).wait_recv()
-
-    def finish_swap(s):
-        swaps[s].wait()
-        parts[s + 1] = parts[s] + inbox[s]
-        if s + 1 < steps:
-            swaps[s + 1].start()
+    y_arrive()
+    finish_swap(0)
+    sibling_arrive()
 
     oc = 512
     back = []
-    done_swaps = 0
+    done_swaps = 1
     for t in range(tiles):
         for d in range(1, n):
             j = lax.rem(me + d, n)
@@ -167,22 +237,23 @@
             return carry
 
         lax.fori_loop(0, orient // oc, penalty, 0)
+        rsend[t] = racc[...].astype(BF)
+        rrecv[t, me] = rsend[t, me]
+        for d in range(1, n):
+            j = lax.rem(me + d, n)
+            item = remote(rsend.at[t, j], rrecv.at[t, me], gsend.at[t, d], grecv.at[t, me], j)
+            item.start()
+            back.append(item)
         if done_swaps < steps:
             finish_swap(done_swaps)
             done_swaps += 1
-        rsend[t] = racc[...].astype(BF)
-        rrecv[t, me] = rsend[t, me]
-        for d in range(1, n):
-            j = lax.rem(me + d, n)
-            item = remote(rsend.at[t, j], rrecv.at[t, me], gsend.at[t, d], grecv.at[t, me], j)
-            item.start()
-            back.append(item)
-    while done_swaps < steps:
+    while done_swaps <= steps:
         finish_swap(done_swaps)
         done_swaps += 1
 
     loads[3].wait()
-    resid_ref[...] = parts[steps] - meas[...]
+    full[mine] = half[steps - 1]
+    resid_ref[...] = full[...] - meas[...]
     for z in range(layers):
         for a in range(angles):
             bp_t[:, a * nrays:(a + 1) * nrays] = dot(
@@ -209,7 +280,7 @@
                                          out_sem.at[t, d])
             item.start()
             outs.append(item)
-    for item in harm_direct + [harm_sib] + forwards + coef_copies + back:
+    for item in sent + coef_copies + back + swaps:
         item.wait_send()
     for item in outs:
         item.wait()
@@ -217,6 +288,10 @@
 
 def body(coefficients, measured, ray_voxels, ray_weights, angle_ids, angle_table, harmonics):
     n = lax.axis_size("coef")
+    slabs = lax.axis_size("slab")
+    split = lax.axis_size("groups")
+    if (harmonics.shape[1] // (slabs * split)) % LANES:
+        split = 1
     cl, width = coefficients.shape
     angles, layers, nrays, chans = measured.shape
     rows = angles * nrays
@@ -230,7 +305,7 @@
     smem_spec = pl.BlockSpec(memory_space=pltpu.SMEM)
     dma = pltpu.SemaphoreType.DMA
     updated, residual = pl.pallas_call(
-        functools.partial(kernel, n, tiles),
+        functools.partial(kernel, n, slabs, split, tiles),
         out_shape=(jax.ShapeDtypeStruct(coefficients.shape, F32),
                    jax.ShapeDtypeStruct(measured.shape, F32)),
         in_specs=[any_spec, any_spec, vmem_spec, vmem_spec, smem_spec, any_spec, any_spec],
@@ -246,20 +321,30 @@
             pltpu.VMEM((16 * (NG * NG // LANES), LANES), F32),
             pltpu.VMEM((rows, cl), BF),
             pltpu.VMEM((rows, cl), F32),
-            pltpu.VMEM((steps + 1,) + measured.shape, F32),
-            pltpu.VMEM((steps,) + measured.shape, F32),
+            pltpu.VMEM(measured.shape, F32),
+            pltpu.VMEM((steps, angles // 2) + measured.shape[1:], F32),
+            pltpu.VMEM((steps, angles // 2) + measured.shape[1:], F32),
+            pltpu.VMEM(measured.shape, F32),
             pltpu.VMEM((cl, rows), BF),
             pltpu.VMEM((n, cl, vt), F32),
             pltpu.VMEM((tiles, n, cl, vt), BF),
             pltpu.VMEM((tiles, n, cl, vt), BF),
             dma((4,)),
             dma((tiles, n)),
-            dma((2, n)),
+            dma((1,)),
+            dma((1,)),
             dma((n,)),
-            dma((tiles, n)),
-            dma((tiles, n)),
-            dma((steps,)),
-            dma((steps,)),
+            dma((n,)),
+            dma((n, slabs)),
+            dma((n, slabs)),
+            dma((n, slabs, split)),
+            dma((n, slabs, split)),
+            dma((n, slabs, split)),
+            dma((n, slabs, split)),
+            dma((tiles, n)),
+            dma((tiles, n)),
+            dma((steps + 1,)),
+            dma((steps + 1,)),
             dma((tiles, n)),
             dma((tiles, n)),
         ],

time: 84.7 us -> 70.2 us (0.83)
  Pallas kernels: 77.1 us -> 63.3 us
    pallas_call x1, Pallas kernels: 77.1 us -> 63.3 us  [body(): pl.pallas_call(functools.partial(kernel, n, slabs, split, tiles), out_sha...]
where the time goes in v2:
time: 70.2 us; the launch traced here: 70 us
  Pallas kernels  63.3 us (90%)
  local copies, waits for them, and re-layouts  6.07 us (9%)
    pallas_call x1, Pallas kernels, body(): pl.pallas_call(functools.partial(kernel, n, slabs, split, tiles), out_sha...  63.3 us
    unnamed x1, local copies, waits for them, and re-layouts  4.28 us
    dynamic_slice x1, local copies, waits for them, and re-layouts, body(): lax.dynamic_slice_in_dim(residual, lax.axis_index('coef') * chan_width, c...  1.8 us

profile of v2, /device:TPU:9, one launch (start us, length us, event | category | flops | bytes accessed | tf_op | source)
XLA Modules:
  0.0 70.0 jit_solution(7562895049651652203)
XLA Ops:
  0.6 63.3 %step.1 = (f32[224,4096]{1,0:T(8,128)}, f32[8,1,64,256]{3,2,1,0:T(8,128)}) custom-call(f32[224,4096]{1,0:T(8,128)} %coef_hbm.1, f32[8,1,64,256]{3,2,1,0:T(8,128)} %meas_hbm.1, s32[512,128]{1,0:T(8,128)} %bitcast.2, s32[512,128]{1,0:T(8,128)} %bitcast.3, s32[8]{0:T(128)} %ids_ref.1, bf16[16,224,256]{2,1,0:T(8,128)(2,1)} %table_hbm.1, bf16[224,2048]{1,0:T(8,128)(2,1)} %harm_hbm.1), custom_call_target="tpu_custom_call" | custom-call | tf_op jit(solution)/shard_map/step/pallas_call | solution.py:307
  64.0 1.8 %constant_dynamic-slice_fusion = f32[8,1,64,64]{3,2,1,0:T(8,128)} fusion(f32[8,1,64,256]{3,2,1,0:T(8,128)} %get-tuple-element.5, s32[]{:T(128)S(6)} %select_n.3), kind=kLoop, calls=%fused_computation | loop fusion | bytes 262148 | tf_op jit(solution)/shard_map/dynamic_slice | solution.py:357
  65.8 4.3 %copy.10 = f32[224,4096]{1,0:T(8,128)} copy(f32[224,4096]{1,0:T(8,128)} %get-tuple-element.8) | data formatting | bytes 7340032

commit v3 on v2

--- a/solution.py
+++ b/solution.py
@@ -22,9 +22,9 @@
 
 def kernel(n, slabs, split, tiles, coef_hbm, meas_hbm, vox_ref, wgt_ref, ids_ref, table_hbm, harm_hbm,
            upd_hbm, resid_ref,
-           coef, coef_bf, meas, table, harm, recv, matrix, prod, rays, ray_acc, part, half, inbox, full,
+           coef, coef_bf, meas, table, harm, recv, matrix, prod, rays, ray_acc, part, half, half_bf, inbox, inbox_bf, full,
            bp_t, racc, rsend, rrecv,
-           load_sem, out_sem, own_s, own_r, hx_s, hx_r, hz_s, hz_r, hy_s, hy_r, hs_s, hs_r,
+           load_sem, coef_sem, out_sem, own_s, own_r, hx_s, hx_r, hz_s, hz_r, hy_s, hy_r, hs_s, hs_r,
            csend, crecv, psend, precv, gsend, grecv):
     me = lax.axis_index("coef")
     mz = lax.axis_index("slab")
@@ -38,12 +38,20 @@
     steps = n.bit_length() - 1
     sibling = me + 1 - 2 * lax.rem(me, 2)
 
+    mates = [lax.rem(me + 2 * e, n) for e in range(1, n // 2)]
+    sib_mates = [lax.rem(sibling + 2 * e, n) for e in range(1, n // 2)]
+    targets = mates + sib_mates + [sibling]
+    blocks = []
+    for d, j in enumerate(targets + [me]):
+        at = pl.ds(pl.multiple_of(j * share, LANES), share)
+        blocks.append(pltpu.make_async_copy(coef_hbm.at[:, at], coef.at[:, at], coef_sem.at[d]))
     loads = [
-        pltpu.make_async_copy(coef_hbm, coef, load_sem.at[0]),
-        pltpu.make_async_copy(harm_hbm, harm.at[me], load_sem.at[1]),
-        pltpu.make_async_copy(table_hbm, table, load_sem.at[2]),
-        pltpu.make_async_copy(meas_hbm, meas, load_sem.at[3]),
+        pltpu.make_async_copy(harm_hbm, harm.at[me], load_sem.at[0]),
+        pltpu.make_async_copy(table_hbm, table, load_sem.at[1]),
+        pltpu.make_async_copy(meas_hbm, meas, load_sem.at[2]),
     ]
+    for item in blocks:
+        item.start()
     for item in loads:
         item.start()
 
@@ -60,8 +68,6 @@
             device_id={axis: target}, device_id_type=pl.DeviceIdType.MESH)
 
     ow = orient // (slabs * split)
-    mates = [lax.rem(me + 2 * e, n) for e in range(1, n // 2)]
-    sib_mates = [lax.rem(sibling + 2 * e, n) for e in range(1, n // 2)]
     sent = []
 
     def cols(zi, yi):
@@ -123,24 +129,39 @@
                 for yi in range(split):
                     arrived(harm.at[b, :, cols(zi, yi)], hs_r.at[b, zi, yi])
 
-    loads[0].wait()
     coef_copies = []
+    far = len(targets) - 1
+
+    def span(j, t):
+        return pl.ds(pl.multiple_of(j * share + t * vt, LANES), vt)
+
+    def cast(d, t):
+        j = (targets + [me])[d]
+        if t == 0:
+            blocks[d].wait()
+        coef_bf[:, span(j, t)] = coef[:, span(j, t)].astype(BF)
+
+    def send(d, t):
+        j = targets[d]
+        item = remote(coef_bf.at[:, span(j, t)], recv.at[t, me], csend.at[t, d], crecv.at[t, me], j)
+        item.start()
+        coef_copies.append(item)
+
+    for d in range(far):
+        cast(d, 0)
+    for d in range(far):
+        send(d, 0)
+    cast(far, 0)
+    for t in range(1, tiles):
+        for d in range(far + 1):
+            cast(d, t)
+        for d in range(far):
+            send(d, t)
     for t in range(tiles):
-        for d in range(n):
-            j = lax.rem(me + d, n)
-            at = pl.multiple_of(j * share + t * vt, LANES)
-            block = coef[:, pl.ds(at, vt)].astype(BF)
-            coef_bf[:, pl.ds(at, vt)] = block
-            if d == 0:
-                recv[t, me] = block
+        send(far, t)
     for t in range(tiles):
-        for d in range(1, n):
-            j = lax.rem(me + d, n)
-            at = pl.multiple_of(j * share + t * vt, LANES)
-            item = remote(coef_bf.at[:, pl.ds(at, vt)], recv.at[t, me], csend.at[t, d],
-                          crecv.at[t, me], j)
-            item.start()
-            coef_copies.append(item)
+        cast(far + 1, t)
+        recv[t, me] = coef_bf[:, span(me, t)]
 
     samples = vox_ref.shape[1]
     rows_hi = plane // LANES
@@ -173,60 +194,16 @@
     for q in range(parts, slabs):
         z_arrive(q)
 
-    kc = 512
-    loads[2].wait()
-    for z in range(layers):
-        ray_acc[...] = jnp.zeros_like(ray_acc)
-
-        def project(i, carry, z=z):
-            at = pl.multiple_of(i * kc, kc)
-            ray_acc[...] += dot(matrix[:, pl.ds(at, kc)],
-                                coef_bf[:, pl.ds(pl.multiple_of(z * plane + i * kc, kc), kc)], NT)
-            return carry
-
-        lax.fori_loop(0, plane // kc, project, 0)
-        rays[...] = ray_acc[...].astype(BF)
-        for a in range(angles):
-            part[a, z] = dot(rays[a * nrays:(a + 1) * nrays, :], table[ids_ref[a]], NN)
-
-    ha = angles // 2
-    par = lax.rem(me, 2)
-    mine, other = pl.ds(par * ha, ha), pl.ds((1 - par) * ha, ha)
-
-    def swap(s):
-        if s == 0:
-            return remote(part.at[other], inbox.at[0], psend.at[0], precv.at[0], sibling)
-        if s == steps:
-            return remote(half.at[s - 1], full.at[mine], psend.at[s], precv.at[s], sibling)
-        bit = 1 << s
-        partner = me + (1 - 2 * lax.rem(me // bit, 2)) * bit
-        return remote(half.at[s - 1], inbox.at[s], psend.at[s], precv.at[s], partner)
-
-    swaps = [swap(s) for s in range(steps + 1)]
-    swaps[0].start()
-
-    def finish_swap(s):
-        swaps[s].wait_recv()
-        if s < steps:
-            half[s] = (part[mine] if s == 0 else half[s - 1]) + inbox[s]
-            swaps[s + 1].start()
-
-    loads[1].wait()
-    y_arrive()
-    finish_swap(0)
-    sibling_arrive()
-
     oc = 512
     back = []
-    done_swaps = 1
-    for t in range(tiles):
+
+    def penalty_tile(t):
         for d in range(1, n):
             j = lax.rem(me + d, n)
-            remote(coef_bf.at[:, pl.ds(0, vt)], recv.at[t, j], csend.at[t, d],
-                   crecv.at[t, j], j).wait_recv()
+            arrived(recv.at[t, j], crecv.at[t, j])
         racc[...] = jnp.zeros_like(racc)
 
-        def penalty(i, carry, t=t):
+        def penalty(i, carry):
             at = pl.multiple_of(i * oc, oc)
             field = dot(harm[0, :, pl.ds(at, oc)], recv[t, 0], TN)
             for j in range(1, n):
@@ -239,11 +216,66 @@
         lax.fori_loop(0, orient // oc, penalty, 0)
         rsend[t] = racc[...].astype(BF)
         rrecv[t, me] = rsend[t, me]
-        for d in range(1, n):
-            j = lax.rem(me + d, n)
+        for d, j in enumerate(targets):
             item = remote(rsend.at[t, j], rrecv.at[t, me], gsend.at[t, d], grecv.at[t, me], j)
             item.start()
             back.append(item)
+
+    early = 0
+    for t in range(early):
+        penalty_tile(t)
+
+    kc = 512
+    loads[1].wait()
+    for z in range(layers):
+        ray_acc[...] = jnp.zeros_like(ray_acc)
+
+        def project(i, carry, z=z):
+            at = pl.multiple_of(i * kc, kc)
+            ray_acc[...] += dot(matrix[:, pl.ds(at, kc)],
+                                coef_bf[:, pl.ds(pl.multiple_of(z * plane + i * kc, kc), kc)], NT)
+            return carry
+
+        lax.fori_loop(0, plane // kc, project, 0)
+        rays[...] = ray_acc[...].astype(BF)
+        for a in range(angles):
+            part[a, z] = dot(rays[a * nrays:(a + 1) * nrays, :], table[ids_ref[a]], NN)
+
+    ha = angles // 2
+    par = lax.rem(me, 2)
+    mine, other = pl.ds(par * ha, ha), pl.ds((1 - par) * ha, ha)
+
+    def swap(s):
+        if s == 0:
+            return remote(part.at[other], inbox.at[0], psend.at[0], precv.at[0], sibling)
+        if s == steps:
+            return remote(half.at[s - 1], full.at[mine], psend.at[s], precv.at[s], sibling)
+        bit = 1 << s
+        partner = me + (1 - 2 * lax.rem(me // bit, 2)) * bit
+        return remote(half_bf.at[s - 1], inbox_bf.at[s - 1], psend.at[s], precv.at[s], partner)
+
+    swaps = [swap(s) for s in range(steps + 1)]
+    swaps[0].start()
+
+    def finish_swap(s):
+        swaps[s].wait_recv()
+        if s < steps:
+            if s == 0:
+                half[s] = part[mine] + inbox[0]
+            else:
+                half[s] = half[s - 1] + inbox_bf[s - 1].astype(F32)
+            if s + 1 < steps:
+                half_bf[s] = half[s].astype(BF)
+            swaps[s + 1].start()
+
+    loads[0].wait()
+    y_arrive()
+    finish_swap(0)
+    sibling_arrive()
+
+    done_swaps = 1
+    for t in range(early, tiles):
+        penalty_tile(t)
         if done_swaps < steps:
             finish_swap(done_swaps)
             done_swaps += 1
@@ -251,13 +283,19 @@
         finish_swap(done_swaps)
         done_swaps += 1
 
-    loads[3].wait()
+    loads[2].wait()
     full[mine] = half[steps - 1]
-    resid_ref[...] = full[...] - meas[...]
+    full[...] = full[...] - meas[...]
+    cw = chans // n
+    for c in range(n):
+        @pl.when(me == c)
+        def _(c=c):
+            resid_ref[...] = full[:, :, :, c * cw:(c + 1) * cw]
+
     for z in range(layers):
         for a in range(angles):
             bp_t[:, a * nrays:(a + 1) * nrays] = dot(
-                table[ids_ref[a]], resid_ref[a, z].astype(BF), NT).astype(BF)
+                table[ids_ref[a]], full[a, z].astype(BF), NT).astype(BF)
 
         def gradient(i, carry, z=z):
             at = pl.multiple_of(i * kc, kc)
@@ -270,16 +308,13 @@
 
     outs = []
     for t in range(tiles):
-        for d in range(n):
-            j = lax.rem(me + d, n)
-            if d > 0:
-                remote(rsend.at[t, j], rrecv.at[t, j], gsend.at[t, d], grecv.at[t, j], j).wait_recv()
-            at = pl.multiple_of(j * share + t * vt, LANES)
-            coef[:, pl.ds(at, vt)] = coef[:, pl.ds(at, vt)] - 0.5 * rrecv[t, j].astype(F32)
-            item = pltpu.make_async_copy(coef.at[:, pl.ds(at, vt)], upd_hbm.at[:, pl.ds(at, vt)],
-                                         out_sem.at[t, d])
-            item.start()
-            outs.append(item)
+        for d, j in enumerate([me] + targets):
+            if j is not me:
+                arrived(rrecv.at[t, j], grecv.at[t, j])
+            coef[:, span(j, t)] = coef[:, span(j, t)] - 0.5 * rrecv[t, j].astype(F32)
+            outs.append(pltpu.make_async_copy(coef.at[:, span(j, t)], upd_hbm.at[:, span(j, t)],
+                                              out_sem.at[t, d]))
+            outs[-1].start()
     for item in sent + coef_copies + back + swaps:
         item.wait_send()
     for item in outs:
@@ -300,16 +335,16 @@
     tiles = 2
     vt = share // tiles
     steps = n.bit_length() - 1
-    any_spec = pl.BlockSpec(memory_space=pl.ANY)
+    any_spec = pl.BlockSpec(memory_space=pltpu.HBM)
     vmem_spec = pl.BlockSpec(memory_space=pltpu.VMEM)
     smem_spec = pl.BlockSpec(memory_space=pltpu.SMEM)
     dma = pltpu.SemaphoreType.DMA
     updated, residual = pl.pallas_call(
         functools.partial(kernel, n, slabs, split, tiles),
         out_shape=(jax.ShapeDtypeStruct(coefficients.shape, F32),
-                   jax.ShapeDtypeStruct(measured.shape, F32)),
+                   jax.ShapeDtypeStruct((angles, layers, nrays, chans // n), F32)),
         in_specs=[any_spec, any_spec, vmem_spec, vmem_spec, smem_spec, any_spec, any_spec],
-        out_specs=(any_spec, vmem_spec),
+        out_specs=(pl.BlockSpec(memory_space=pl.ANY), vmem_spec),
         scratch_shapes=[
             pltpu.VMEM((cl, width), F32),
             pltpu.VMEM((cl, width), BF),
@@ -323,13 +358,16 @@
             pltpu.VMEM((rows, cl), F32),
             pltpu.VMEM(measured.shape, F32),
             pltpu.VMEM((steps, angles // 2) + measured.shape[1:], F32),
-            pltpu.VMEM((steps, angles // 2) + measured.shape[1:], F32),
+            pltpu.VMEM((max(steps - 1, 1), angles // 2) + measured.shape[1:], BF),
+            pltpu.VMEM((1, angles // 2) + measured.shape[1:], F32),
+            pltpu.VMEM((max(steps - 1, 1), angles // 2) + measured.shape[1:], BF),
             pltpu.VMEM(measured.shape, F32),
             pltpu.VMEM((cl, rows), BF),
             pltpu.VMEM((n, cl, vt), F32),
             pltpu.VMEM((tiles, n, cl, vt), BF),
             pltpu.VMEM((tiles, n, cl, vt), BF),
-            dma((4,)),
+            dma((3,)),
+            dma((n,)),
             dma((tiles, n)),
             dma((1,)),
             dma((1,)),
@@ -353,8 +391,6 @@
         name="step",
     )(coefficients, measured, ray_voxels.reshape(rows, -1), ray_weights.reshape(rows, -1),
       angle_ids, angle_table, harmonics)
-    chan_width = chans // n
-    residual = lax.dynamic_slice_in_dim(residual, lax.axis_index("coef") * chan_width, chan_width, 3)
     return updated, residual
 
 

time: 70.2 us -> 69.7 us (level)
  local copies, waits for them, and re-layouts: 6.07 us -> 5.03 us
    dynamic_slice x1 -> x0, local copies, waits for them, and re-layouts: 1.8 us -> none  [body(): lax.dynamic_slice_in_dim(residual, lax.axis_index('coef') * chan_width, c...]
    unnamed x1 -> x4, local copies, waits for them, and re-layouts: 4.28 us -> 5.03 us
where the time goes in v3:
time: 69.7 us; the launch traced here: 69.2 us
  Pallas kernels  63.5 us (91%)
  local copies, waits for them, and re-layouts  5.03 us (7%)
    pallas_call x1, Pallas kernels, body(): pl.pallas_call(functools.partial(kernel, n, slabs, split, tiles), out_sha...  63.5 us
    unnamed x4, local copies, waits for them, and re-layouts  5.03 us

profile of v3, /device:TPU:9, one launch (start us, length us, event | category | flops | bytes accessed | tf_op | source)
XLA Modules:
  0.0 69.2 jit_solution(1957554080709057619)
XLA Ops:
  0.6 63.5 %step.1 = (f32[224,4096]{1,0:T(8,128)}, f32[8,1,64,64]{3,2,1,0:T(8,128)}) custom-call(f32[224,4096]{1,0:T(8,128)} %coef_hbm.1, f32[8,1,64,256]{3,2,1,0:T(8,128)} %meas_hbm.1, s32[512,128]{1,0:T(8,128)} %bitcast.2, s32[512,128]{1,0:T(8,128)} %bitcast.3, s32[8]{0:T(128)} %ids_ref.1, bf16[16,224,256]{2,1,0:T(8,128)(2,1)} %table_hbm.1, bf16[224,2048]{1,0:T(8,128)(2,1)} %harm_hbm.1), custom_call_target="tpu_custom_call" | custom-call | tf_op jit(solution)/shard_map/step/pallas_call | solution.py:342
  64.2 0.0 copy-start
  64.2 4.3 %copy.11 = f32[224,4096]{1,0:T(8,128)} copy(f32[224,4096]{1,0:T(8,128)} %get-tuple-element.4) | data formatting | bytes 7340032
  68.5 0.0 copy-done
  68.5 0.7 %copy.12 = f32[8,1,64,64]{3,2,1,0:T(8,128)} copy(f32[8,1,64,64]{3,2,1,0:T(8,128)S(1)} %copy-done) | data formatting | bytes 262144
Async XLA Ops:
  64.2 4.3 %copy-start = (f32[8,1,64,64]{3,2,1,0:T(8,128)S(1)}, f32[8,1,64,64]{3,2,1,0:T(8,128)}, u32[]{:S(2)}) copy-start(f32[8,1,64,64]{3,2,1,0:T(8,128)} %get-tuple-element.5) | copy-start | bytes 393220
